TPU v7x, 128 devices: a whole 4x4x4 slice. The times are simulated.
128 devices in a mesh: wide: 8 (over y, core), narrow: 16 (over z, x).
Axes of the slice: x: 4, y: 4, z: 4, core: 2. Of those that a mesh axis runs over, the one named last changes fastest.
Arguments:
- latent_in: bfloat16 [2048, 1024], P(('wide', 'narrow')), may hold values from -6 to 6
- latent_grad: bfloat16 [2048, 1024], P(('wide', 'narrow')), may hold values from -6 to 6
- route_ids: int32 [2048, 22], P(('wide', 'narrow')), may hold values from 0 to 127, all different within a row; in each aligned block of 16 rows (0 to 15, 16 to 31, ...) at most 8 rows name the same one
- gate_values: float32 [2048, 22], P(('wide', 'narrow')), may hold values from 0.05 to 1
- up_weight: bfloat16 [128, 1024, 2688], P(('wide', 'narrow')), may hold values from -0.1875 to 0.1875
- down_weight: bfloat16 [128, 2688, 1024], P(('wide', 'narrow')), may hold values from -0.125 to 0.125
- inputs: bfloat16 [2048, 4096], P('wide', 'narrow'), may hold values from -6 to 6
- proj_weight: bfloat16 [4096, 1024], P('narrow'), may hold values from -0.09375 to 0.09375
Outputs:
- grad_up: bfloat16 [128, 1024, 2688], P(('wide', 'narrow'))
- grad_down: bfloat16 [128, 2688, 1024], P(('wide', 'narrow'))
- grad_inputs: bfloat16 [2048, 4096], P('wide', 'narrow')
- grad_proj: float32 [4096, 1024], P('narrow', 'wide')
Inputs may be any that keep to these rules, and one draw needn't show every extreme that they name: `route_ids`: each token names 22 different experts; among the 16 tokens of one device no expert is named by more than 8 tokens, a bound that some block reaches.
All inputs are finite; a program needn't handle non-finite values.
Results may differ from a plain program's by a relative error of at most 0.015.
Values may be sent and summed in bfloat16 or wider, within the bound.
No kernel may reach another device: no remote copies, remote signals or barrier semaphores. Data moves between devices by JAX's collectives and lax.ppermute only.
A program may use at most 128 MiB of HBM per device.

v0:
```python
import jax
import jax.numpy as jnp
from jax import lax
from jax.sharding import PartitionSpec as P


def expert_pass(z_rows, dy_rows, w_up, w_down):
    hidden = jnp.dot(z_rows, w_up, preferred_element_type=jnp.float32)
    active = jnp.maximum(hidden, 0.0)
    squared = (active * active).astype(jnp.bfloat16)
    act_grad = lax.dot_general(
        dy_rows, w_down, (((1,), (1,)), ((), ())), preferred_element_type=jnp.float32
    )
    hid_grad = (act_grad * 2.0 * active).astype(jnp.bfloat16)
    row_grad = lax.dot_general(
        hid_grad, w_up, (((1,), (1,)), ((), ())), preferred_element_type=jnp.float32
    ).astype(jnp.bfloat16)
    down_part = lax.dot_general(
        squared, dy_rows, (((0,), (0,)), ((), ())), preferred_element_type=jnp.float32
    )
    up_part = lax.dot_general(
        z_rows, hid_grad, (((0,), (0,)), ((), ())), preferred_element_type=jnp.float32
    )
    return (row_grad, up_part, down_part)


def on_device(
    latent_in, latent_grad, route_ids, gate_values, up_weight, down_weight, inputs, proj_weight
):
    n_wide = lax.axis_size("wide")
    n_narrow = lax.axis_size("narrow")
    experts = n_wide * n_narrow
    token_count, top_count = route_ids.shape
    width = latent_in.shape[1]
    capacity = min(token_count, max(8, 2 * ((token_count * top_count + experts - 1) // experts)))
    flat_routes = route_ids.reshape(-1)
    pairs = flat_routes.shape[0]
    route_hits = (flat_routes[:, None] == jnp.arange(experts, dtype=jnp.int32)[None, :]).astype(
        jnp.int32
    )
    slot_rank = jnp.sum((jnp.cumsum(route_hits, axis=0) - route_hits) * route_hits, axis=1)
    slot_index = flat_routes * capacity + slot_rank
    pair_token = jnp.arange(pairs, dtype=jnp.int32) // top_count
    source_token = (
        jnp.full((experts * capacity,), token_count, jnp.int32).at[slot_index].set(pair_token)
    )
    slot_gate = (
        jnp.zeros((experts * capacity,), jnp.float32).at[slot_index].set(gate_values.reshape(-1))
    )
    empty_row = jnp.zeros((1, width), jnp.bfloat16)
    send_z = jnp.take(jnp.concatenate([latent_in, empty_row]), source_token, axis=0)
    send_dy = (
        jnp.take(jnp.concatenate([latent_grad, empty_row]), source_token, axis=0).astype(
            jnp.float32
        )
        * slot_gate[:, None]
    ).astype(jnp.bfloat16)
    recv_z, recv_dy = (
        lax.all_to_all(
            send_z.reshape(experts, capacity, width),
            ("wide", "narrow"),
            split_axis=0,
            concat_axis=0,
            tiled=True,
        ),
        lax.all_to_all(
            send_dy.reshape(experts, capacity, width),
            ("wide", "narrow"),
            split_axis=0,
            concat_axis=0,
            tiled=True,
        ),
    )
    flat_z = recv_z.reshape(-1, width)
    flat_dy = recv_dy.reshape(-1, width)
    row_grad, up_part, down_part = expert_pass(flat_z, flat_dy, up_weight[0], down_weight[0])
    returned = lax.all_to_all(
        row_grad.reshape(experts, capacity, width),
        ("wide", "narrow"),
        split_axis=0,
        concat_axis=0,
        tiled=True,
    )
    pair_rows = jnp.take(returned.reshape(experts * capacity, width), slot_index, axis=0)
    token_grad = jnp.sum(
        pair_rows.reshape(token_count, top_count, width).astype(jnp.float32), axis=1
    ).astype(jnp.bfloat16)
    piece = lax.all_gather(token_grad, "narrow", axis=0, tiled=True)
    proj_acc = lax.dot_general(
        inputs, piece, (((0,), (0,)), ((), ())), preferred_element_type=jnp.float32
    )
    input_part = lax.dot_general(
        piece, proj_weight, (((1,), (1,)), ((), ())), preferred_element_type=jnp.float32
    )
    input_acc = input_part
    proj_acc, input_acc = (proj_acc, input_acc)
    grad_proj = lax.psum_scatter(proj_acc, "wide", scatter_dimension=1, tiled=True)
    grad_up = up_part.astype(jnp.bfloat16)[None]
    grad_down = down_part.astype(jnp.bfloat16)[None]
    return (grad_up, grad_down, input_acc.astype(jnp.bfloat16), grad_proj)


def solution(mesh):
    placed = (
        P(("wide", "narrow"), None),
        P(("wide", "narrow"), None),
        P(("wide", "narrow"), None),
        P(("wide", "narrow"), None),
        P(("wide", "narrow"), None, None),
        P(("wide", "narrow"), None, None),
        P("wide", "narrow"),
        P("narrow", None),
    )
    return jax.shard_map(
        on_device,
        mesh=mesh,
        in_specs=placed,
        out_specs=(
            P(("wide", "narrow"), None, None),
            P(("wide", "narrow"), None, None),
            P("wide", "narrow"),
            P("narrow", "wide"),
        ),
        check_vma=False,
    )
```

profile of v0, /device:TPU:1, one launch (start us, length us, event | category | flops | bytes accessed | tf_op | source)
XLA Modules:
  0.0 214.0 jit_solution(16302143375772465826)
XLA Ops:
  7.2 0.0 copy-start
  7.2 0.8 eq.22
  8.0 0.7 broadcast_multiply_fusion
  8.7 0.1 mul.44
  8.8 0.1 iota_compare_fusion
  9.0 0.1 fusion.15
  9.2 0.1 broadcast_add_fusion
  9.2 0.2 fusion.18
  9.5 2.9 %scatter_custom_fusion = s32[1024]{0:T(1024)S(1)} fusion(s32[352]{0:T(512)S(1)} %fusion.27, s32[352]{0:T(512)S(1)} %add_select_fusion, s32[]{:T(128)} %constant.29.clone.1), kind=kCustom, calls=%fused_computation.54 | custom fusion | bytes 4100 | tf_op jit(solution)/shard_map/scatter | solution.py:45
  12.5 0.8 concatenate.6
  13.2 4.1 %gather_fusion.1 = bf16[1024,1024]{1,0:T(8,128)(2,1)S(1)} fusion(bf16[17,1024]{1,0:T(8,128)(2,1)S(1)} %concatenate.6, s32[1024]{0:T(1024)S(1)} %fusion.19), kind=kCustom, calls=%fused_computation.clone | custom fusion | bytes 4198400 | tf_op jit(solution)/shard_map/jit(_take)/gather | solution.py:51
  17.3 0.0 copy-start.5
  17.3 0.0 copy-start.4
  17.3 1.6 select_bitcast_fusion
  18.9 11.9 %all-to-all-start = ((bf16[128,8,1024]{2,1,0:T(8,128)(2,1)}), bf16[128,8,1024]{2,1,0:T(8,128)(2,1)}, u32[]{:S(2)}, u32[]{:S(2)}) async-start(bf16[128,8,1024]{2,1,0:T(8,128)(2,1)} %select_bitcast_fusion), calls=%async_computation | async-start | bytes 4194304 | tf_op jit(solution)/shard_map/all_to_all | solution.py:59
  30.8 0.1 reduce_sum.27
  30.9 0.0 copy-done.5
  30.9 0.1 reshape.136
  31.0 0.0 copy-done.4
  31.1 4.1 %gather_fusion.2 = bf16[1024,1024]{1,0:T(8,128)(2,1)S(1)} fusion(bf16[17,1024]{1,0:T(8,128)(2,1)S(1)} %concatenate.7, s32[1024]{0:T(1024)S(1)} %fusion.19), kind=kCustom, calls=%fused_computation.1.clone | custom fusion | bytes 4198400 | tf_op jit(solution)/shard_map/jit(_take)/gather | solution.py:53
  35.1 0.0 copy-start.3
  35.1 2.9 %scatter_custom_fusion.1 = f32[1024]{0:T(1024)S(1)} fusion(s32[352]{0:T(512)S(1)} %fusion.27, f32[352]{0:T(512)S(1)} %reshape.136, f32[]{:T(128)} %constant.54.clone.1), kind=kCustom, calls=%fused_computation.52 | custom fusion | bytes 4100 | tf_op jit(solution)/shard_map/scatter | solution.py:48
  38.1 1.9 fusion.8
  40.0 20.0 %all-to-all-done = bf16[128,8,1024]{2,1,0:T(8,128)(2,1)} async-done(((bf16[128,8,1024]{2,1,0:T(8,128)(2,1)}), bf16[128,8,1024]{2,1,0:T(8,128)(2,1)}, u32[]{:S(2)}, u32[]{:S(2)}) %all-to-all-start) | async-done | bytes 2097184 | tf_op jit(solution)/shard_map/all_to_all | solution.py:59
  59.9 4.9 %all-to-all-start.1 = ((bf16[128,8,1024]{2,1,0:T(8,128)(2,1)}), bf16[128,8,1024]{2,1,0:T(8,128)(2,1)S(1)}, u32[]{:S(2)}, u32[]{:S(2)}) async-start(bf16[128,8,1024]{2,1,0:T(8,128)(2,1)} %fusion.8), calls=%async_computation.1 | async-start | bytes 4194304 | tf_op jit(solution)/shard_map/all_to_all | solution.py:66
  64.8 0.0 copy-done.3
  64.8 11.7 %fusion.2 = f32[1024,2688]{1,0:T(8,128)} fusion(bf16[1,1024,2688]{2,1,0:T(8,128)(2,1)} %param.14, bf16[128,8,1024]{2,1,0:T(8,128)(2,1)} %all-to-all-done), kind=kOutput, calls=%fused_computation.11 | convolution fusion | flops 5637144576 | bytes 18612224 | tf_op jit(solution)/shard_map/dot_general | solution.py:8
  76.5 17.8 %all-to-all-done.1 = bf16[128,8,1024]{2,1,0:T(8,128)(2,1)S(1)} async-done(((bf16[128,8,1024]{2,1,0:T(8,128)(2,1)}), bf16[128,8,1024]{2,1,0:T(8,128)(2,1)S(1)}, u32[]{:S(2)}, u32[]{:S(2)}) %all-to-all-start.1) | async-done | bytes 2097184 | tf_op jit(solution)/shard_map/all_to_all | solution.py:66
  94.3 0.0 copy-start.1
  94.3 11.4 %multiply_convert_fusion.1 = bf16[1024,2688]{1,0:T(8,128)(2,1)S(1)} fusion(f32[1024,2688]{1,0:T(8,128)} %fusion.2, bf16[1,2688,1024]{2,1,0:T(8,128)(2,1)} %param.15, bf16[128,8,1024]{2,1,0:T(8,128)(2,1)S(1)} %all-to-all-done.1), kind=kOutput, calls=%fused_computation.6 | convolution fusion | flops 5648154624 | bytes 24117248 | tf_op jit(solution)/shard_map/dot_general | solution.py:11
  105.8 0.0 copy-done.1
  105.8 0.0 copy-start.6
  105.8 2.3 %copy-done.6 = bf16[1024,2688]{1,0:T(8,128)(2,1)} copy-done((bf16[1024,2688]{1,0:T(8,128)(2,1)}, bf16[1024,2688]{1,0:T(8,128)(2,1)S(1)}, u32[]{:S(2)}) %copy-start.6) | copy-done | bytes 5505048
  108.1 9.2 %convert_bitcast_fusion = bf16[128,8,1024]{2,1,0:T(8,128)(2,1)} fusion(bf16[1024,2688]{1,0:T(8,128)(2,1)S(1)} %multiply_convert_fusion.1, bf16[1,1024,2688]{2,1,0:T(8,128)(2,1)} %param.14), kind=kOutput, calls=%fused_computation.24 | convolution fusion | flops 5638193152 | bytes 13107200 | tf_op jit(solution)/shard_map/dot_general | solution.py:15
  117.3 4.9 %all-to-all-start.2 = ((bf16[128,8,1024]{2,1,0:T(8,128)(2,1)}), bf16[128,8,1024]{2,1,0:T(8,128)(2,1)S(1)}, u32[]{:S(2)}, u32[]{:S(2)}) async-start(bf16[128,8,1024]{2,1,0:T(8,128)(2,1)} %convert_bitcast_fusion), calls=%async_computation.2 | async-start | bytes 4194304 | tf_op jit(solution)/shard_map/all_to_all | solution.py:77
  122.2 0.0 reduce-scatter.2.cloned.1.call-start
  122.2 12.2 %fusion.7 = bf16[1,2688,1024]{2,1,0:T(8,128)(2,1)} fusion(f32[1024,2688]{1,0:T(8,128)} %fusion.2, bf16[128,8,1024]{2,1,0:T(8,128)(2,1)} %copy-done.1), kind=kOutput, calls=%fused_computation.16 | convolution fusion | flops 5648154624 | bytes 18612224 | tf_op jit(solution)/shard_map/dot_general | solution.py:18
  134.4 0.0 copy-start.2
  134.4 17.3 %all-to-all-done.2 = bf16[128,8,1024]{2,1,0:T(8,128)(2,1)S(1)} async-done(((bf16[128,8,1024]{2,1,0:T(8,128)(2,1)}), bf16[128,8,1024]{2,1,0:T(8,128)(2,1)S(1)}, u32[]{:S(2)}, u32[]{:S(2)}) %all-to-all-start.2) | async-done | bytes 2097184 | tf_op jit(solution)/shard_map/all_to_all | solution.py:77
  151.7 2.1 gather_fusion
  153.9 0.2 gather.10
  154.1 0.3 select_reduce_fusion
  154.3 18.1 %all_gather.3 = bf16[256,1024]{1,0:T(8,128)(2,1)S(1)} all-gather(bf16[16,1024]{1,0:T(8,128)(2,1)S(1)} %select_reduce_fusion), channel_id=1, replica_groups=mesh['wide'=8,'narrow'=16] {'narrow'}, dimensions={0}, use_global_device_ids=true | all-gather | bytes 557056 | tf_op jit(solution)/shard_map/all_gather | solution.py:88
  172.5 0.0 copy-done.2
  172.5 1.3 convolution_bitcast_fusion
  173.8 0.0 reduce-scatter.2.cloned.1.call-update
  173.8 10.9 %fusion.6 = bf16[1,1024,2688]{2,1,0:T(8,128)(2,1)} fusion(bf16[1024,2688]{1,0:T(8,128)(2,1)} %copy-done.6, bf16[128,8,1024]{2,1,0:T(8,128)(2,1)} %all-to-all-done), kind=kOutput, calls=%fused_computation.15 | convolution fusion | flops 5639897088 | bytes 13107200 | tf_op jit(solution)/shard_map/dot_general | solution.py:21
  184.7 0.0 copy-done
  184.7 1.0 convolution_convert_fusion.2
  185.7 19.9 %reduce-scatter.2.cloned.1.call-done = f32[256,128]{0,1:T(8,128)} async-done(((f32[256,1024]{0,1:T(8,128)}), f32[256,128]{0,1:T(8,128)}) %reduce-scatter.2.cloned.1.call-update) | async-done | bytes 131088 | tf_op jit(solution)/shard_map/reduce_scatter | solution.py:97
  205.5 1.7 copy.15
  (11 shorter events, 0.1 us)
Async XLA Ops:
  7.2 177.5 %copy-start = (bf16[256,1024]{1,0:T(8,128)(2,1)S(1)}, bf16[256,1024]{1,0:T(8,128)(2,1)}, u32[]{:S(2)}) copy-start(bf16[256,1024]{1,0:T(8,128)(2,1)} %param.17) | copy-start | bytes 1572868
  17.3 13.7 %copy-start.5 = (f32[16,22]{1,0:T(8,128)S(1)}, f32[16,22]{1,0:T(8,128)}, u32[]{:S(2)}) copy-start(f32[16,22]{1,0:T(8,128)} %param.13) | copy-start | bytes 4228
  17.3 13.7 %copy-start.4 = (bf16[16,1024]{1,0:T(8,128)(2,1)S(1)}, bf16[16,1024]{1,0:T(8,128)(2,1)}, u32[]{:S(2)}) copy-start(bf16[16,1024]{1,0:T(8,128)(2,1)} %param.11) | copy-start | bytes 98308
  18.9 41.0 %all-to-all-start = ((bf16[128,8,1024]{2,1,0:T(8,128)(2,1)}), bf16[128,8,1024]{2,1,0:T(8,128)(2,1)}, u32[]{:S(2)}, u32[]{:S(2)}) async-start(bf16[128,8,1024]{2,1,0:T(8,128)(2,1)} %select_bitcast_fusion), calls=%async_computation | async-start | bytes 4194304 | tf_op jit(solution)/shard_map/all_to_all | solution.py:59
  35.1 29.7 %copy-start.3 = (s32[16,22]{1,0:T(8,128)S(1)}, s32[16,22]{1,0:T(8,128)}, u32[]{:S(2)}) copy-start(s32[16,22]{1,0:T(8,128)} %param.12) | copy-start | bytes 4228
  59.9 34.4 %all-to-all-start.1 = ((bf16[128,8,1024]{2,1,0:T(8,128)(2,1)}), bf16[128,8,1024]{2,1,0:T(8,128)(2,1)S(1)}, u32[]{:S(2)}, u32[]{:S(2)}) async-start(bf16[128,8,1024]{2,1,0:T(8,128)(2,1)} %fusion.8), calls=%async_computation.1 | async-start | bytes 4194304 | tf_op jit(solution)/shard_map/all_to_all | solution.py:66
  94.3 11.4 %copy-start.1 = (bf16[128,8,1024]{2,1,0:T(8,128)(2,1)}, bf16[128,8,1024]{2,1,0:T(8,128)(2,1)S(1)}, u32[]{:S(2)}) copy-start(bf16[128,8,1024]{2,1,0:T(8,128)(2,1)S(1)} %all-to-all-done.1) | copy-start | bytes 6291460
  105.8 2.4 %copy-start.6 = (bf16[1024,2688]{1,0:T(8,128)(2,1)}, bf16[1024,2688]{1,0:T(8,128)(2,1)S(1)}, u32[]{:S(2)}) copy-start(bf16[1024,2688]{1,0:T(8,128)(2,1)S(1)} %multiply_convert_fusion.1) | copy-start | bytes 16515076
  117.3 34.4 %all-to-all-start.2 = ((bf16[128,8,1024]{2,1,0:T(8,128)(2,1)}), bf16[128,8,1024]{2,1,0:T(8,128)(2,1)S(1)}, u32[]{:S(2)}, u32[]{:S(2)}) async-start(bf16[128,8,1024]{2,1,0:T(8,128)(2,1)} %convert_bitcast_fusion), calls=%async_computation.2 | async-start | bytes 4194304 | tf_op jit(solution)/shard_map/all_to_all | solution.py:77
  122.2 83.4 %reduce-scatter.2.cloned.1.call-start = ((), (), s32[]{:S(2)}) async-start(), calls=%async_computation.4 | async-start | bytes 1179648 | tf_op jit(solution)/shard_map/reduce_scatter | solution.py:97
  134.4 38.1 %copy-start.2 = (bf16[256,256]{1,0:T(8,128)(2,1)S(1)}, bf16[256,256]{1,0:T(8,128)(2,1)}, u32[]{:S(2)}) copy-start(bf16[256,256]{1,0:T(8,128)(2,1)} %param.16) | copy-start | bytes 393220
Sparse Core Ops, SparseCore 0:
  173.9 31.5 reduce-scatter.1
where the time goes:
time: 217 us; the launch traced here: 214 us
  waiting for transfers between devices  75 us (35%)
  matrix products  57.6 us (27%)
  local copies, waits for them, and re-layouts  22.2 us (10%)
  starting transfers between devices  21.7 us (10%)
  blocking collectives  18.1 us (8%)
  between operations  14.3 us (7%)
  other arithmetic  5.09 us (2%)
    all_to_all x1, waiting for transfers between devices, on_device(): lax.all_to_all(send_z.reshape(experts, capacity, width), ('wide', 'narrow...  20 us
    reduce_scatter x1, waiting for transfers between devices, on_device(): lax.psum_scatter(proj_acc, 'wide', scatter_dimension=1, tiled=True)  19.9 us
    all_gather x1, blocking collectives, on_device(): piece = lax.all_gather(token_grad, 'narrow', axis=0, tiled=True)  18.1 us
    all_to_all x1, waiting for transfers between devices, on_device(): lax.all_to_all(send_dy.reshape(experts, capacity, width), ('wide', 'narro...  17.8 us
    all_to_all x1, waiting for transfers between devices, on_device(): lax.all_to_all(row_grad.reshape(experts, capacity, width), ('wide', 'narr...  17.3 us
    dot_general x1, matrix products, expert_pass(): lax.dot_general(squared, dy_rows, (((0,), (0,)), ((), ())), preferred_ele...  12.2 us
    all_to_all x1, starting transfers between devices, on_device(): lax.all_to_all(send_z.reshape(experts, capacity, width), ('wide', 'narrow...  11.9 us
    dot_general x1, matrix products, expert_pass(): hidden = jnp.dot(z_rows, w_up, preferred_element_type=jnp.float32)  11.7 us
  transfers between devices with their start and end apart: 4, of which 4 were waited for; matrix products, arithmetic and copies ran while one was open for 21% of the time, Pallas kernels for 0%

commit v1 on v0

v1 whole, which is shorter than its diff:
```python
import functools

import jax
import jax.numpy as jnp
from jax import lax
from jax.experimental import pallas as pl
from jax.experimental.pallas import tpu as pltpu
from jax.sharding import PartitionSpec as P

BF16 = jnp.bfloat16
F32 = jnp.float32
SLOTS = 8
PAD_MARK = 64.0
BLOCK = 512
VMEM_LIMIT = 56 * 1024 * 1024


def dot(a, b, dims, **kw):
    return lax.dot_general(a, b, (dims, ((), ())), preferred_element_type=F32, **kw)


NN = ((1,), (0,))
NT = ((1,), (1,))
TN = ((0,), (0,))


def pack_kernel(route_ref, gate_ref, z_ref, g_ref, send_ref, place_ref, *, rows):
    step = pl.program_id(0)
    tokens, top = route_ref.shape
    experts = 128
    width = z_ref.shape[1]
    routes = route_ref[...]
    gates = gate_ref[...]
    expert_of = lax.broadcasted_iota(jnp.int32, (tokens, experts), 1)
    hits = jnp.zeros((tokens, experts), F32)
    weights = jnp.zeros((tokens, experts), F32)
    for k in range(top):
        same = routes[:, k : k + 1] == expert_of
        hits = jnp.where(same, 1.0, hits)
        weights = jnp.where(same, gates[:, k : k + 1], weights)
    before = lax.broadcasted_iota(jnp.int32, (tokens, tokens), 1) < lax.broadcasted_iota(
        jnp.int32, (tokens, tokens), 0
    )
    rank = dot(before.astype(F32).astype(BF16), hits.astype(BF16), NN)
    rank = jnp.where(hits > 0, rank, -1.0).astype(BF16)
    row = lax.broadcasted_iota(jnp.int32, (rows, experts), 0)
    expert = lax.broadcasted_iota(jnp.int32, (rows, experts), 1)
    spread = jnp.where((row >> 3) + step * (rows // SLOTS) == expert, 1.0, 0.0)
    slot = lax.broadcasted_iota(jnp.int32, (rows, tokens), 0) & (SLOTS - 1)
    chosen = jnp.where(dot(spread.astype(BF16), rank, NT) == slot.astype(F32), 1.0, 0.0)
    gate = jnp.sum(
        chosen * dot(spread, weights, NT, precision=lax.Precision.HIGHEST), axis=1, keepdims=True
    )
    live = jnp.sum(chosen, axis=1, keepdims=True)
    chosen = chosen.astype(BF16)
    z_rows = dot(chosen, z_ref[...], NN)
    lane = lax.broadcasted_iota(jnp.int32, (rows, 128), 1)
    mark = jnp.where(lane == 0, (1.0 - live) * PAD_MARK, 0.0)
    send_ref[:, :128] = (z_rows[:, :128] + mark).astype(BF16)
    send_ref[:, 128:width] = z_rows[:, 128:].astype(BF16)
    send_ref[:, width:] = (dot(chosen, g_ref[...], NN) * gate).astype(BF16)
    slot_t = lax.broadcasted_iota(jnp.int32, (tokens, rows), 1) & (SLOTS - 1)
    place_ref[...] = jnp.where(
        dot(rank, spread.astype(BF16), NT) == slot_t.astype(F32), 1.0, 0.0
    ).astype(BF16)


def pack(routes, gates, z, g):
    tokens, width = z.shape
    total = 128 * SLOTS
    rows = 256
    whole = lambda a: pl.BlockSpec(a.shape, lambda i: (0, 0))
    return pl.pallas_call(
        functools.partial(pack_kernel, rows=rows),
        grid=(total // rows,),
        in_specs=[whole(routes), whole(gates), whole(z), whole(g)],
        out_specs=[
            pl.BlockSpec((rows, 2 * width), lambda i: (i, 0)),
            pl.BlockSpec((tokens, rows), lambda i: (0, i)),
        ],
        out_shape=[
            jax.ShapeDtypeStruct((total, 2 * width), BF16),
            jax.ShapeDtypeStruct((tokens, total), BF16),
        ],
        compiler_params=pltpu.CompilerParams(vmem_limit_bytes=VMEM_LIMIT),
        name="pack",
    )(routes, gates, z, g)


def chunks_of(hidden_units):
    edges = list(range(0, hidden_units, 768)) + [hidden_units]
    return list(zip(edges[:-1], edges[1:]))


def expert_kernel(
    recv_ref, up_hbm, down_hbm, ret_ref, zd_hbm, sq_hbm, hid_hbm, count_ref,
    up, down, zd, sq, hid, row_acc, row_out, pos_col, pos_row, in_sem, out_sem, zd_sem,
):
    total, twice = recv_ref.shape
    width = twice // 2
    chunks = chunks_of(up.shape[1])

    def weight_copies(n):
        a, b = chunks[n]
        return (
            pltpu.make_async_copy(up_hbm.at[:, a:b], up.at[:, a:b], in_sem.at[2 * n]),
            pltpu.make_async_copy(down_hbm.at[a:b, :], down.at[a:b, :], in_sem.at[2 * n + 1]),
        )

    def result_copies(i, n):
        a, b = chunks[n]
        r = slice(i * BLOCK, (i + 1) * BLOCK)
        return (
            pltpu.make_async_copy(sq.at[:, a:b], sq_hbm.at[r, a:b], out_sem.at[2 * n]),
            pltpu.make_async_copy(hid.at[:, a:b], hid_hbm.at[r, a:b], out_sem.at[2 * n + 1]),
        )

    def row_copy(i):
        return pltpu.make_async_copy(zd, zd_hbm.at[i * BLOCK : (i + 1) * BLOCK, :], zd_sem)

    for n in range(len(chunks)):
        for c in weight_copies(n):
            c.start()

    live = jnp.where(recv_ref[:, 0:128].astype(F32)[:, 0:1] < PAD_MARK / 2, 1.0, 0.0)
    live = jnp.broadcast_to(live, (total, 128))
    live_bf = live.astype(BF16)
    part = 256
    for p in range(total // part):
        r = slice(p * part, (p + 1) * part)
        earlier = (
            lax.broadcasted_iota(jnp.int32, (part, total), 1)
            < lax.broadcasted_iota(jnp.int32, (part, total), 0) + p * part
        )
        place = dot(jnp.where(earlier, 1.0, 0.0).astype(BF16), live_bf, NN)
        pos_col[r, :] = jnp.where(live[r, :] > 0, place, -1.0)
    pos_row[...] = pos_col[...].T
    count = jnp.max(pos_col[...]).astype(jnp.int32) + 1
    count_ref[0, 0] = count

    def one_block(i):
        want = (lax.broadcasted_iota(jnp.int32, (BLOCK, total), 0) + i * BLOCK).astype(F32)
        pick = jnp.where(jnp.broadcast_to(pos_row[0:1, :], (BLOCK, total)) == want, 1.0, 0.0)
        zd[...] = dot(pick.astype(BF16), recv_ref[...], NN).astype(BF16)
        row_copy(i).start()
        for n, (a, b) in enumerate(chunks):
            if i == 0:
                for c in weight_copies(n):
                    c.wait()
            active = jnp.maximum(dot(zd[:, :width], up[:, a:b], NN), 0.0)
            sq[:, a:b] = (active * active).astype(BF16)
            act_grad = dot(zd[:, width:], down[a:b, :], NT)
            hid[:, a:b] = (act_grad * 2.0 * active).astype(BF16)
            for c in result_copies(i, n):
                c.start()
            rows = dot(hid[:, a:b], up[:, a:b], NT)
            if n == 0:
                row_acc[...] = rows
            else:
                row_acc[...] += rows
        row_out[i * BLOCK : (i + 1) * BLOCK, :] = row_acc[...].astype(BF16)

    def drain(i):
        row_copy(i).wait()
        for n in range(len(chunks)):
            for c in result_copies(i, n):
                c.wait()

    def give_back(i):
        have = (lax.broadcasted_iota(jnp.int32, (total, BLOCK), 1) + i * BLOCK).astype(F32)
        put = jnp.where(jnp.broadcast_to(pos_col[:, 0:1], (total, BLOCK)) == have, 1.0, 0.0)
        return dot(put.astype(BF16), row_out[i * BLOCK : (i + 1) * BLOCK, :], NN)

    one_block(0)
    ret_ref[...] = give_back(0).astype(BF16)
    drain(0)

    @pl.when(count > BLOCK)
    def _():
        one_block(1)
        ret_ref[...] = (ret_ref[...].astype(F32) + give_back(1)).astype(BF16)
        drain(1)


def expert_pass(recv, up, down):
    total, twice = recv.shape
    width, units = up.shape
    n = len(chunks_of(units))
    vmem = pl.BlockSpec(memory_space=pltpu.VMEM)
    hbm = pl.BlockSpec(memory_space=pl.ANY)
    return pl.pallas_call(
        expert_kernel,
        in_specs=[vmem, hbm, hbm],
        out_specs=[vmem, hbm, hbm, hbm, pl.BlockSpec(memory_space=pltpu.SMEM)],
        out_shape=[
            jax.ShapeDtypeStruct((total, width), BF16),
            jax.ShapeDtypeStruct((total, twice), BF16),
            jax.ShapeDtypeStruct((total, units), BF16),
            jax.ShapeDtypeStruct((total, units), BF16),
            jax.ShapeDtypeStruct((1, 1), jnp.int32),
        ],
        scratch_shapes=[
            pltpu.VMEM((width, units), BF16),
            pltpu.VMEM((units, width), BF16),
            pltpu.VMEM((BLOCK, twice), BF16),
            pltpu.VMEM((BLOCK, units), BF16),
            pltpu.VMEM((BLOCK, units), BF16),
            pltpu.VMEM((BLOCK, width), F32),
            pltpu.VMEM((total, width), BF16),
            pltpu.VMEM((total, 128), F32),
            pltpu.VMEM((128, total), F32),
            pltpu.SemaphoreType.DMA((2 * n,)),
            pltpu.SemaphoreType.DMA((2 * n,)),
            pltpu.SemaphoreType.DMA,
        ],
        compiler_params=pltpu.CompilerParams(vmem_limit_bytes=VMEM_LIMIT),
        name="expert",
    )(recv, up, down)


def weight_kernel(count_ref, zd_ref, sq_ref, hid_ref, up_ref, down_ref):
    width = zd_ref.shape[1] // 2

    def emit(rows):
        down_ref[0] = dot(sq_ref[:rows, :], zd_ref[:rows, width:], TN).astype(BF16)
        up_ref[0] = dot(zd_ref[:rows, :width], hid_ref[:rows, :], TN).astype(BF16)

    @pl.when(count_ref[0, 0] <= BLOCK)
    def _():
        emit(BLOCK)

    @pl.when(count_ref[0, 0] > BLOCK)
    def _():
        emit(2 * BLOCK)


def weight_grads(count, zd, sq, hid):
    total, twice = zd.shape
    width, units = twice // 2, sq.shape[1]
    tile = 384
    return pl.pallas_call(
        weight_kernel,
        grid=(units // tile,),
        in_specs=[
            pl.BlockSpec(memory_space=pltpu.SMEM),
            pl.BlockSpec((total, twice), lambda j: (0, 0)),
            pl.BlockSpec((total, tile), lambda j: (0, j)),
            pl.BlockSpec((total, tile), lambda j: (0, j)),
        ],
        out_specs=[
            pl.BlockSpec((1, width, tile), lambda j: (0, 0, j)),
            pl.BlockSpec((1, tile, width), lambda j: (0, j, 0)),
        ],
        out_shape=[
            jax.ShapeDtypeStruct((1, width, units), BF16),
            jax.ShapeDtypeStruct((1, units, width), BF16),
        ],
        compiler_params=pltpu.CompilerParams(vmem_limit_bytes=VMEM_LIMIT),
        cost_estimate=pl.CostEstimate(
            flops=4 * BLOCK * width * units, transcendentals=0, bytes_accessed=8 * width * units
        ),
        name="weight_grads",
    )(count, zd, sq, hid)


def exchange(x, axes):
    return lax.all_to_all(x, axes, split_axis=0, concat_axis=0, tiled=True)


def on_device(
    latent_in, latent_grad, route_ids, gate_values, up_weight, down_weight, inputs, proj_weight
):
    n_wide = lax.axis_size("wide")
    n_narrow = lax.axis_size("narrow")
    experts = n_wide * n_narrow
    both = ("wide", "narrow")
    tokens, width = latent_in.shape
    send, place = pack(route_ids, gate_values, latent_in, latent_grad)
    recv = exchange(send.reshape(experts, SLOTS, 2 * width), both)
    rows, zd, sq, hid, count = expert_pass(
        recv.reshape(experts * SLOTS, 2 * width), up_weight[0], down_weight[0]
    )
    returned = exchange(rows.reshape(experts, SLOTS, width), both)
    grad_up, grad_down = weight_grads(count, zd, sq, hid)
    returned, grad_up, grad_down = lax.optimization_barrier((returned, grad_up, grad_down))
    token_grad = dot(place, returned.reshape(experts * SLOTS, width), NN).astype(BF16)
    copies = jnp.broadcast_to(token_grad[None], (n_narrow, tokens, width))
    piece = exchange(copies, "narrow").reshape(n_narrow * tokens, width)
    columns = width // n_wide
    parts = dot(inputs, piece, TN).astype(BF16)
    parts = parts.reshape(inputs.shape[1], n_wide, columns).transpose(1, 0, 2)
    parts = exchange(parts, "wide")
    grad_proj = jnp.sum(parts.astype(F32), axis=0)
    grad_inputs = dot(piece, proj_weight, NT).astype(BF16)
    return (grad_up, grad_down, grad_inputs, grad_proj)


def solution(mesh):
    placed = (
        P(("wide", "narrow"), None),
        P(("wide", "narrow"), None),
        P(("wide", "narrow"), None),
        P(("wide", "narrow"), None),
        P(("wide", "narrow"), None, None),
        P(("wide", "narrow"), None, None),
        P("wide", "narrow"),
        P("narrow", None),
    )
    return jax.shard_map(
        on_device,
        mesh=mesh,
        in_specs=placed,
        out_specs=(
            P(("wide", "narrow"), None, None),
            P(("wide", "narrow"), None, None),
            P("wide", "narrow"),
            P("narrow", "wide"),
        ),
        check_vma=False,
    )
```

time: 217 us -> 166 us (0.76)
  blocking collectives: 18.1 us -> 77.4 us
  matrix products: 57.6 us -> 2.53 us
  waiting for transfers between devices: 75 us -> 22.6 us
  Pallas kernels: 0 us -> 38.3 us
  local copies, waits for them, and re-layouts: 22.2 us -> 0.84 us
  between operations: 14.3 us -> 0.69 us
  other arithmetic: 5.09 us -> 0.07 us
    all_to_all x0 -> x2, blocking collectives: none -> 77.4 us  [exchange(): return lax.all_to_all(x, axes, split_axis=0, concat_axis=0, tiled=True)]
    dot_general x7 -> x3, matrix products: 57.6 us -> 2.53 us  [dot(): lax.dot_general(a, b, (dims, ((), ())), preferred_element_type=F32, **kw)]
    pallas_call x0 -> x3, Pallas kernels: none -> 38.3 us  [the longest x1 17.8 us: expert_pass(): pl.pallas_call(expert_kernel, in_specs=[vmem, hbm, hbm], out_specs=[vmem,...]
    all_to_all x3 -> x2, waiting for transfers between devices: 55.1 us -> 22.6 us  [exchange(): return lax.all_to_all(x, axes, split_axis=0, concat_axis=0, tiled=True)]
    reduce_scatter x1 -> x0, waiting for transfers between devices: 19.9 us -> none  [on_device(): lax.psum_scatter(proj_acc, 'wide', scatter_dimension=1, tiled=True)]
    all_gather x1 -> x0, blocking collectives: 18.1 us -> none  [on_device(): piece = lax.all_gather(token_grad, 'narrow', axis=0, tiled=True)]
    gather x4 -> x0, local copies, waits for them, and re-layouts: 10.4 us -> none  [the longest x1 4.07 us: on_device(): jnp.take(jnp.concatenate([latent_grad, empty_row]), source_token, axis=0)]
    scatter x2 -> x0, local copies, waits for them, and re-layouts: 5.85 us -> none  [the longest x1 2.92 us: on_device(): jnp.full((experts * capacity,), token_count, jnp.int32).at[slot_index]]
  transfers between devices with their start and end apart: 4 -> 2, of which waited for: 4 -> 2; matrix products, arithmetic and copies ran while one was open for 21% -> 1% of each run, Pallas kernels for 0% -> 9%
where the time goes in v1:
time: 166 us; the launch traced here: 165 us
  blocking collectives  77.4 us (47%)
  Pallas kernels  38.3 us (23%)
  starting transfers between devices  22.6 us (14%)
  waiting for transfers between devices  22.6 us (14%)
  matrix products  2.53 us (2%)
    all_to_all x2, blocking collectives, exchange(): return lax.all_to_all(x, axes, split_axis=0, concat_axis=0, tiled=True)  77.4 us
    all_to_all x2, waiting for transfers between devices, exchange(): return lax.all_to_all(x, axes, split_axis=0, concat_axis=0, tiled=True)  22.6 us
    all_to_all x2, starting transfers between devices, exchange(): return lax.all_to_all(x, axes, split_axis=0, concat_axis=0, tiled=True)  22.6 us
    pallas_call x1, Pallas kernels, expert_pass(): pl.pallas_call(expert_kernel, in_specs=[vmem, hbm, hbm], out_specs=[vmem,...  17.8 us
    pallas_call x1, Pallas kernels, weight_grads(): pl.pallas_call(weight_kernel, grid=(units // tile,), in_specs=[pl.BlockSp...  15.1 us
    pallas_call x1, Pallas kernels, pack(): pl.pallas_call(functools.partial(pack_kernel, rows=rows), grid=(total //...  5.37 us
  transfers between devices with their start and end apart: 2, of which 2 were waited for; matrix products, arithmetic and copies ran while one was open for 1% of the time, Pallas kernels for 9%

profile of v1, /device:TPU:1, one launch (start us, length us, event | category | flops | bytes accessed | tf_op | source)
XLA Modules:
  0.0 165.1 jit_solution(12629678067230535819)
XLA Ops:
  0.6 0.0 copy-start
  0.6 5.4 %pack.1 = (bf16[1024,2048]{1,0:T(8,128)(2,1)}, bf16[16,1024]{1,0:T(8,128)(2,1)}) custom-call(s32[16,22]{1,0:T(8,128)} %route_ref.1, f32[16,22]{1,0:T(8,128)} %gate_ref.1, bf16[16,1024]{1,0:T(8,128)(2,1)} %z_ref.1, bf16[16,1024]{1,0:T(8,128)(2,1)} %g_ref.1), custom_call_target="tpu_custom_call" | custom-call | tf_op jit(solution)/shard_map/pack/pallas_call | solution.py:73
  6.0 63.1 %all_to_all.20 = bf16[128,8,2048]{2,1,0:T(8,128)(2,1)} all-to-all(bf16[128,8,2048]{2,1,0:T(8,128)(2,1)} %bitcast.26), channel_id=1, replica_groups=mesh['wide'=8,'narrow'=16] {'wide','narrow'}, dimensions={0} | all-to-all | bytes 8388608 | tf_op jit(solution)/shard_map/all_to_all | solution.py:267
  69.1 17.8 %expert.1 = (bf16[1024,1024]{1,0:T(8,128)(2,1)}, bf16[1024,2048]{1,0:T(8,128)(2,1)}, bf16[1024,2688]{1,0:T(8,128)(2,1)}, bf16[1024,2688]{1,0:T(8,128)(2,1)}, s32[1,1]{1,0:T(1,128)}) custom-call(bf16[1024,2048]{1,0:T(8,128)(2,1)} %bitcast.21, bf16[1024,2688]{1,0:T(8,128)(2,1)} %bitcast.22, bf16[2688,1024]{1,0:T(8,128)(2,1)} %bitcast.23), custom_call_target="tpu_custom_call" | custom-call | tf_op jit(solution)/shard_map/expert/pallas_call | solution.py:191
  87.0 17.3 %all-to-all-start.1 = ((bf16[128,8,1024]{2,1,0:T(8,128)(2,1)}), bf16[128,8,1024]{2,1,0:T(8,128)(2,1)S(1)}, u32[]{:S(2)}, u32[]{:S(2)}) async-start(bf16[128,8,1024]{2,1,0:T(8,128)(2,1)} %bitcast.27), calls=%async_computation.1 | async-start | bytes 4194304 | tf_op jit(solution)/shard_map/all_to_all | solution.py:267
  104.3 0.0 copy-start.2
  104.3 0.0 copy-start.1
  104.3 15.1 %weight_grads.1 = (bf16[1,1024,2688]{2,1,0:T(8,128)(2,1)}, bf16[1,2688,1024]{2,1,0:T(8,128)(2,1)}) custom-call(s32[1,1]{1,0:T(1,128)} %get-tuple-element.18.count_ref, bf16[1024,2048]{1,0:T(8,128)(2,1)} %get-tuple-element.19.zd_ref, bf16[1024,2688]{1,0:T(8,128)(2,1)} %get-tuple-element.20.sq_ref, bf16[1024,2688]{1,0:T(8,128)(2,1)} %get-tuple-element.21.hid_ref), custom_call_target="tpu_custom_call" | custom-call | flops 5637144576 | bytes 22020096 | tf_op jit(solution)/shard_map/weight_grads/pallas_call | solution.py:241
  119.4 14.3 %all-to-all-done.1 = bf16[128,8,1024]{2,1,0:T(8,128)(2,1)S(1)} async-done(((bf16[128,8,1024]{2,1,0:T(8,128)(2,1)}), bf16[128,8,1024]{2,1,0:T(8,128)(2,1)S(1)}, u32[]{:S(2)}, u32[]{:S(2)}) %all-to-all-start.1) | async-done | bytes 2097184 | tf_op jit(solution)/shard_map/all_to_all | solution.py:267
  133.7 0.0 copy-done.2
  133.7 0.4 fusion.2
  134.1 0.1 broadcast_in_dim.2
  134.1 14.2 %all_to_all.21 = bf16[16,16,1024]{2,1,0:T(8,128)(2,1)S(1)} all-to-all(bf16[16,16,1024]{2,1,0:T(8,128)(2,1)S(1)} %broadcast_in_dim.2), channel_id=1, replica_groups=mesh['wide'=8,'narrow'=16] {'narrow'}, dimensions={0} | all-to-all | bytes 1048576 | tf_op jit(solution)/shard_map/all_to_all | solution.py:267
  148.4 0.0 copy-done.1
  148.4 1.1 convolution_convert_fusion
  149.5 5.3 %all-to-all-start.3 = ((bf16[8,256,128]{1,2,0:T(8,128)(2,1)}), bf16[8,256,128]{1,2,0:T(8,128)(2,1)S(1)}, u32[]{:S(2)}, u32[]{:S(2)}) async-start(bf16[8,256,128]{1,2,0:T(8,128)(2,1)} %bitcast.9), calls=%async_computation.3 | async-start | bytes 1048576 | tf_op jit(solution)/shard_map/all_to_all | solution.py:267
  154.8 0.0 copy-done
  154.9 1.0 convolution_convert_fusion.1
  155.8 8.4 %all-to-all-done.3 = bf16[8,256,128]{1,2,0:T(8,128)(2,1)S(1)} async-done(((bf16[8,256,128]{1,2,0:T(8,128)(2,1)}), bf16[8,256,128]{1,2,0:T(8,128)(2,1)S(1)}, u32[]{:S(2)}, u32[]{:S(2)}) %all-to-all-start.3) | async-done | bytes 524320 | tf_op jit(solution)/shard_map/all_to_all | solution.py:267
  164.2 0.1 convert_reduce_fusion
  164.3 0.8 copy.12
Async XLA Ops:
  0.6 154.2 %copy-start = (bf16[256,1024]{1,0:T(8,128)(2,1)S(1)}, bf16[256,1024]{1,0:T(8,128)(2,1)}, u32[]{:S(2)}) copy-start(bf16[256,1024]{1,0:T(8,128)(2,1)} %param.15) | copy-start | bytes 1572868
  87.0 46.7 %all-to-all-start.1 = ((bf16[128,8,1024]{2,1,0:T(8,128)(2,1)}), bf16[128,8,1024]{2,1,0:T(8,128)(2,1)S(1)}, u32[]{:S(2)}, u32[]{:S(2)}) async-start(bf16[128,8,1024]{2,1,0:T(8,128)(2,1)} %bitcast.27), calls=%async_computation.1 | async-start | bytes 4194304 | tf_op jit(solution)/shard_map/all_to_all | solution.py:267
  104.3 29.4 %copy-start.2 = (bf16[16,1024]{1,0:T(8,128)(2,1)S(1)}, bf16[16,1024]{1,0:T(8,128)(2,1)}, u32[]{:S(2)}) copy-start(bf16[16,1024]{1,0:T(8,128)(2,1)} %get-tuple-element.26) | copy-start | bytes 98308
  104.3 44.1 %copy-start.1 = (bf16[256,256]{1,0:T(8,128)(2,1)S(1)}, bf16[256,256]{1,0:T(8,128)(2,1)}, u32[]{:S(2)}) copy-start(bf16[256,256]{1,0:T(8,128)(2,1)} %param.14) | copy-start | bytes 393220
  149.5 14.7 %all-to-all-start.3 = ((bf16[8,256,128]{1,2,0:T(8,128)(2,1)}), bf16[8,256,128]{1,2,0:T(8,128)(2,1)S(1)}, u32[]{:S(2)}, u32[]{:S(2)}) async-start(bf16[8,256,128]{1,2,0:T(8,128)(2,1)} %bitcast.9), calls=%async_computation.3 | async-start | bytes 1048576 | tf_op jit(solution)/shard_map/all_to_all | solution.py:267

commit v2 on v1

v2 whole, which is shorter than its diff:
```python
import functools

import jax
import jax.numpy as jnp
from jax import lax
from jax.experimental import pallas as pl
from jax.experimental.pallas import tpu as pltpu
from jax.sharding import PartitionSpec as P

BF16 = jnp.bfloat16
F32 = jnp.float32
SLOTS = 8
BLOCK = 512
PACK_STEPS = 4
VMEM_LIMIT = 56 * 1024 * 1024


def dot(a, b, dims, **kw):
    return lax.dot_general(a, b, (dims, ((), ())), preferred_element_type=F32, **kw)


NN = ((1,), (0,))
NT = ((1,), (1,))
TN = ((0,), (0,))


def pack_kernel(route_ref, gate_ref, z_ref, g_ref, send_hbm, place_ref, send, sem):
    tokens, top = route_ref.shape
    experts = 128
    total, twice = send.shape
    width = twice // 2
    routes = route_ref[...]
    gates = gate_ref[...]
    expert_of = lax.broadcasted_iota(jnp.int32, (tokens, experts), 1)
    hits = jnp.zeros((tokens, experts), F32)
    weights = jnp.zeros((tokens, experts), F32)
    for k in range(top):
        same = routes[:, k : k + 1] == expert_of
        hits = jnp.where(same, 1.0, hits)
        weights = jnp.where(same, gates[:, k : k + 1], weights)
    before = lax.broadcasted_iota(jnp.int32, (tokens, tokens), 1) < lax.broadcasted_iota(
        jnp.int32, (tokens, tokens), 0
    )
    rank = dot(before.astype(F32).astype(BF16), hits.astype(BF16), NN)
    rank = jnp.where(hits > 0, rank, -1.0).astype(BF16)
    rows = total // PACK_STEPS
    copies = []
    for p in range(PACK_STEPS):
        r = slice(p * rows, (p + 1) * rows)
        row = lax.broadcasted_iota(jnp.int32, (rows, experts), 0) + p * rows
        expert = lax.broadcasted_iota(jnp.int32, (rows, experts), 1)
        spread = jnp.where((row >> 3) == expert, 1.0, 0.0)
        spread_bf = spread.astype(BF16)
        slot = lax.broadcasted_iota(jnp.int32, (rows, tokens), 0) & (SLOTS - 1)
        chosen = jnp.where(dot(spread_bf, rank, NT) == slot.astype(F32), 1.0, 0.0)
        gate = jnp.sum(
            chosen * dot(spread, weights, NT, precision=lax.Precision.HIGHEST),
            axis=1,
            keepdims=True,
        )
        chosen = chosen.astype(BF16)
        send[r, :width] = dot(chosen, z_ref[...], NN).astype(BF16)
        send[r, width:] = (dot(chosen, g_ref[...], NN) * gate).astype(BF16)
        copies.append(pltpu.make_async_copy(send.at[r, :], send_hbm.at[r, :], sem.at[p]))
        copies[-1].start()
        slot_t = lax.broadcasted_iota(jnp.int32, (tokens, rows), 1) & (SLOTS - 1)
        place_ref[:, r] = jnp.where(
            dot(rank, spread_bf, NT) == slot_t.astype(F32), 1.0, 0.0
        ).astype(BF16)
    for c in copies:
        c.wait()


def pack(routes, gates, z, g):
    tokens, width = z.shape
    total = 128 * SLOTS
    vmem = pl.BlockSpec(memory_space=pltpu.VMEM)
    return pl.pallas_call(
        pack_kernel,
        in_specs=[vmem] * 4,
        out_specs=[pl.BlockSpec(memory_space=pl.ANY), vmem],
        out_shape=[
            jax.ShapeDtypeStruct((total, 2 * width), BF16),
            jax.ShapeDtypeStruct((tokens, total), BF16),
        ],
        scratch_shapes=[
            pltpu.VMEM((total, 2 * width), BF16),
            pltpu.SemaphoreType.DMA((PACK_STEPS,)),
        ],
        compiler_params=pltpu.CompilerParams(vmem_limit_bytes=VMEM_LIMIT),
        name="pack",
    )(routes, gates, z, g)


def chunks_of(hidden_units):
    sizes = (256, 768, 768, 512)
    edges = [0]
    for size in sizes:
        edges.append(edges[-1] + size)
    edges.append(hidden_units)
    return list(zip(edges[:-1], edges[1:]))


def expert_kernel(
    recv_hbm, up_hbm, down_hbm, ret_hbm, sq_hbm, hid_hbm,
    recv, up, down, sq, hid, row_acc, row_out, recv_sem, up_sem, down_sem, sq_sem, hid_sem, ret_sem,
):
    total, twice = recv.shape
    width = twice // 2
    chunks = chunks_of(up.shape[1])
    blocks = total // BLOCK

    def rows_of(i):
        return slice(i * BLOCK, (i + 1) * BLOCK)

    def copy_recv(i, half):
        at = (rows_of(i), slice(half * width, (half + 1) * width))
        return pltpu.make_async_copy(recv_hbm.at[at], recv.at[at], recv_sem.at[2 * i + half])

    def copy_up(n):
        at = (slice(None), slice(*chunks[n]))
        return pltpu.make_async_copy(up_hbm.at[at], up.at[at], up_sem.at[n])

    def copy_down(n):
        at = (slice(*chunks[n]), slice(None))
        return pltpu.make_async_copy(down_hbm.at[at], down.at[at], down_sem.at[n])

    def copy_out(i, n):
        at = (rows_of(i), slice(*chunks[n]))
        k = i * len(chunks) + n
        return (
            pltpu.make_async_copy(sq.at[at], sq_hbm.at[at], sq_sem.at[k]),
            pltpu.make_async_copy(hid.at[at], hid_hbm.at[at], hid_sem.at[k]),
        )

    def copy_ret(i):
        return pltpu.make_async_copy(row_out.at[rows_of(i)], ret_hbm.at[rows_of(i)], ret_sem.at[i])

    copy_up(0).start()
    copy_recv(0, 0).start()
    copy_down(0).start()
    copy_recv(0, 1).start()
    for n in range(1, len(chunks)):
        copy_up(n).start()
        copy_down(n).start()
    for i in range(1, blocks):
        copy_recv(i, 0).start()
        copy_recv(i, 1).start()
    for i in range(blocks):
        r = rows_of(i)
        copy_recv(i, 0).wait()
        for n, (a, b) in enumerate(chunks):
            if i == 0:
                copy_up(n).wait()
            active = jnp.maximum(dot(recv[r, :width], up[:, a:b], NN), 0.0)
            sq[r, a:b] = (active * active).astype(BF16)
            if n == 0:
                copy_recv(i, 1).wait()
            if i == 0:
                copy_down(n).wait()
            act_grad = dot(recv[r, width:], down[a:b, :], NT)
            hid[r, a:b] = (act_grad * 2.0 * active).astype(BF16)
            for c in copy_out(i, n):
                c.start()
            rows = dot(hid[r, a:b], up[:, a:b], NT)
            if n == 0:
                row_acc[...] = rows
            elif n < len(chunks) - 1:
                row_acc[...] += rows
            else:
                row_out[r, :] = (row_acc[...] + rows).astype(BF16)
        copy_ret(i).start()
    for i in range(blocks):
        for n in range(len(chunks)):
            for c in copy_out(i, n):
                c.wait()
        copy_ret(i).wait()


def expert_pass(recv, up, down):
    total, twice = recv.shape
    width, units = up.shape
    n = len(chunks_of(units))
    blocks = total // BLOCK
    hbm = pl.BlockSpec(memory_space=pl.ANY)
    dma = pltpu.SemaphoreType.DMA
    return pl.pallas_call(
        expert_kernel,
        in_specs=[hbm] * 3,
        out_specs=[hbm] * 3,
        out_shape=[
            jax.ShapeDtypeStruct((total, width), BF16),
            jax.ShapeDtypeStruct((total, units), BF16),
            jax.ShapeDtypeStruct((total, units), BF16),
        ],
        scratch_shapes=[
            pltpu.VMEM((total, twice), BF16),
            pltpu.VMEM((width, units), BF16),
            pltpu.VMEM((units, width), BF16),
            pltpu.VMEM((total, units), BF16),
            pltpu.VMEM((total, units), BF16),
            pltpu.VMEM((BLOCK, width), F32),
            pltpu.VMEM((total, width), BF16),
            dma((2 * blocks,)),
            dma((n,)),
            dma((n,)),
            dma((blocks * n,)),
            dma((blocks * n,)),
            dma((blocks,)),
        ],
        compiler_params=pltpu.CompilerParams(vmem_limit_bytes=VMEM_LIMIT),
        name="expert",
    )(recv, up, down)


def weight_kernel(zd_ref, sq_ref, hid_ref, up_ref, down_ref):
    width = zd_ref.shape[1] // 2
    down_ref[0] = dot(sq_ref[...], zd_ref[:, width:], TN).astype(BF16)
    up_ref[0] = dot(zd_ref[:, :width], hid_ref[...], TN).astype(BF16)


def weight_grads(zd, sq, hid):
    total, twice = zd.shape
    width, units = twice // 2, sq.shape[1]
    tile = 384
    return pl.pallas_call(
        weight_kernel,
        grid=(units // tile,),
        in_specs=[
            pl.BlockSpec((total, twice), lambda j: (0, 0)),
            pl.BlockSpec((total, tile), lambda j: (0, j)),
            pl.BlockSpec((total, tile), lambda j: (0, j)),
        ],
        out_specs=[
            pl.BlockSpec((1, width, tile), lambda j: (0, 0, j)),
            pl.BlockSpec((1, tile, width), lambda j: (0, j, 0)),
        ],
        out_shape=[
            jax.ShapeDtypeStruct((1, width, units), BF16),
            jax.ShapeDtypeStruct((1, units, width), BF16),
        ],
        compiler_params=pltpu.CompilerParams(vmem_limit_bytes=VMEM_LIMIT),
        cost_estimate=pl.CostEstimate(
            flops=4 * total * width * units, transcendentals=0, bytes_accessed=8 * width * units
        ),
        name="weight_grads",
    )(zd, sq, hid)


def part_kernel(inputs_ref, piece_ref, parts_ref):
    n_parts, _, columns = parts_ref.shape
    acc = dot(inputs_ref[...], piece_ref[...], TN)
    for p in range(n_parts):
        parts_ref[p] = acc[:, p * columns : (p + 1) * columns].astype(BF16)


def proj_parts(inputs, piece, n_parts):
    vmem = pl.BlockSpec(memory_space=pltpu.VMEM)
    return pl.pallas_call(
        part_kernel,
        in_specs=[vmem, vmem],
        out_specs=vmem,
        out_shape=jax.ShapeDtypeStruct(
            (n_parts, inputs.shape[1], piece.shape[1] // n_parts), BF16
        ),
        name="proj_parts",
    )(inputs, piece)


def exchange(x, axes):
    return lax.all_to_all(x, axes, split_axis=0, concat_axis=0, tiled=True)


def on_device(
    latent_in, latent_grad, route_ids, gate_values, up_weight, down_weight, inputs, proj_weight
):
    n_wide = lax.axis_size("wide")
    n_narrow = lax.axis_size("narrow")
    experts = n_wide * n_narrow
    both = ("wide", "narrow")
    tokens, width = latent_in.shape
    send, place = pack(route_ids, gate_values, latent_in, latent_grad)
    recv = exchange(send.reshape(experts, SLOTS, 2 * width), both)
    recv = recv.reshape(experts * SLOTS, 2 * width)
    rows, sq, hid = expert_pass(recv, up_weight[0], down_weight[0])
    returned = exchange(rows.reshape(experts, SLOTS, width), both)
    grad_up, grad_down = weight_grads(recv, sq, hid)
    returned, grad_up, grad_down = lax.optimization_barrier((returned, grad_up, grad_down))
    token_grad = dot(place, returned.reshape(experts * SLOTS, width), NN).astype(BF16)
    copies = jnp.broadcast_to(token_grad[None], (n_narrow, tokens, width))
    piece = exchange(copies, "narrow").reshape(n_narrow * tokens, width)
    parts = exchange(proj_parts(inputs, piece, n_wide), "wide")
    grad_proj = jnp.sum(parts.astype(F32), axis=0)
    grad_inputs = dot(piece, proj_weight, NT).astype(BF16)
    return (grad_up, grad_down, grad_inputs, grad_proj)


def solution(mesh):
    placed = (
        P(("wide", "narrow"), None),
        P(("wide", "narrow"), None),
        P(("wide", "narrow"), None),
        P(("wide", "narrow"), None),
        P(("wide", "narrow"), None, None),
        P(("wide", "narrow"), None, None),
        P("wide", "narrow"),
        P("narrow", None),
    )
    return jax.shard_map(
        on_device,
        mesh=mesh,
        in_specs=placed,
        out_specs=(
            P(("wide", "narrow"), None, None),
            P(("wide", "narrow"), None, None),
            P("wide", "narrow"),
            P("narrow", "wide"),
        ),
        check_vma=False,
    )
```

time: 166 us -> 162 us (0.976)
  Pallas kernels: 38.3 us -> 51.3 us
  starting transfers between devices: 22.6 us -> 10.4 us
  waiting for transfers between devices: 22.6 us -> 18.3 us
    all_to_all x2, starting transfers between devices: 22.6 us -> 10.4 us  [exchange(): return lax.all_to_all(x, axes, split_axis=0, concat_axis=0, tiled=True)]
    pallas_call x2 -> x3, Pallas kernels: 23.2 us -> 32.9 us  [the longest x1 25.9 us: expert_pass(): pl.pallas_call(expert_kernel, in_specs=[hbm] * 3, out_specs=[hbm] * 3, ou...]
    all_to_all x2, waiting for transfers between devices: 22.6 us -> 18.3 us  [exchange(): return lax.all_to_all(x, axes, split_axis=0, concat_axis=0, tiled=True)]
    pallas_call x1, Pallas kernels: 15.1 us -> 18.4 us  [weight_grads(): pl.pallas_call(weight_kernel, grid=(units // tile,), in_specs=[pl.BlockSp...]
  transfers between devices with their start and end apart: 2 -> 2, of which waited for: 2 -> 2; matrix products, arithmetic and copies ran while one was open for 1% -> 1% of each run, Pallas kernels for 9% -> 11%
where the time goes in v2:
time: 162 us; the launch traced here: 161 us
  blocking collectives  77.5 us (48%)
  Pallas kernels  51.3 us (32%)
  waiting for transfers between devices  18.3 us (11%)
  starting transfers between devices  10.4 us (6%)
  matrix products  2.42 us (1%)
    all_to_all x2, blocking collectives, exchange(): return lax.all_to_all(x, axes, split_axis=0, concat_axis=0, tiled=True)  77.5 us
    pallas_call x1, Pallas kernels, expert_pass(): pl.pallas_call(expert_kernel, in_specs=[hbm] * 3, out_specs=[hbm] * 3, ou...  25.9 us
    pallas_call x1, Pallas kernels, weight_grads(): pl.pallas_call(weight_kernel, grid=(units // tile,), in_specs=[pl.BlockSp...  18.4 us
    all_to_all x2, waiting for transfers between devices, exchange(): return lax.all_to_all(x, axes, split_axis=0, concat_axis=0, tiled=True)  18.3 us
    all_to_all x2, starting transfers between devices, exchange(): return lax.all_to_all(x, axes, split_axis=0, concat_axis=0, tiled=True)  10.4 us
    pallas_call x1, Pallas kernels, pack(): pl.pallas_call(pack_kernel, in_specs=[vmem] * 4, out_specs=[pl.BlockSpec(...  4.75 us
  transfers between devices with their start and end apart: 2, of which 2 were waited for; matrix products, arithmetic and copies ran while one was open for 1% of the time, Pallas kernels for 11%

profile of v2, /device:TPU:1, one launch (start us, length us, event | category | flops | bytes accessed | tf_op | source)
XLA Modules:
  0.0 161.4 jit_solution(17086717161270460229)
XLA Ops:
  0.6 0.0 copy-start
  0.6 4.7 %pack.1 = (bf16[1024,2048]{1,0:T(8,128)(2,1)}, bf16[16,1024]{1,0:T(8,128)(2,1)}) custom-call(s32[16,22]{1,0:T(8,128)} %route_ref.1, f32[16,22]{1,0:T(8,128)} %gate_ref.1, bf16[16,1024]{1,0:T(8,128)(2,1)} %z_ref.1, bf16[16,1024]{1,0:T(8,128)(2,1)} %g_ref.1), custom_call_target="tpu_custom_call" | custom-call | tf_op jit(solution)/shard_map/pack/pallas_call | solution.py:78
  5.4 63.1 %all_to_all.20 = bf16[128,8,2048]{2,1,0:T(8,128)(2,1)} all-to-all(bf16[128,8,2048]{2,1,0:T(8,128)(2,1)} %bitcast.20), channel_id=1, replica_groups=mesh['wide'=8,'narrow'=16] {'wide','narrow'}, dimensions={0} | all-to-all | bytes 8388608 | tf_op jit(solution)/shard_map/all_to_all | solution.py:271
  68.5 25.9 %expert.1 = (bf16[1024,1024]{1,0:T(8,128)(2,1)}, bf16[1024,2688]{1,0:T(8,128)(2,1)}, bf16[1024,2688]{1,0:T(8,128)(2,1)}) custom-call(bf16[1024,2048]{1,0:T(8,128)(2,1)} %bitcast.14, bf16[1024,2688]{1,0:T(8,128)(2,1)} %bitcast.16, bf16[2688,1024]{1,0:T(8,128)(2,1)} %bitcast.17), custom_call_target="tpu_custom_call" | custom-call | tf_op jit(solution)/shard_map/expert/pallas_call | solution.py:187
  94.4 5.1 %all-to-all-start.1 = ((bf16[128,8,1024]{2,1,0:T(8,128)(2,1)}), bf16[128,8,1024]{2,1,0:T(8,128)(2,1)S(1)}, u32[]{:S(2)}, u32[]{:S(2)}) async-start(bf16[128,8,1024]{2,1,0:T(8,128)(2,1)} %bitcast.21), calls=%async_computation.1 | async-start | bytes 4194304 | tf_op jit(solution)/shard_map/all_to_all | solution.py:271
  99.5 0.0 copy-start.1
  99.5 18.4 %weight_grads.1 = (bf16[1,1024,2688]{2,1,0:T(8,128)(2,1)}, bf16[1,2688,1024]{2,1,0:T(8,128)(2,1)}) custom-call(bf16[1024,2048]{1,0:T(8,128)(2,1)} %bitcast.15, bf16[1024,2688]{1,0:T(8,128)(2,1)} %get-tuple-element.16.sq_ref, bf16[1024,2688]{1,0:T(8,128)(2,1)} %get-tuple-element.17.hid_ref), custom_call_target="tpu_custom_call" | custom-call | flops 11274289152 | bytes 22020096 | tf_op jit(solution)/shard_map/weight_grads/pallas_call | solution.py:226
  117.9 11.0 %all-to-all-done.1 = bf16[128,8,1024]{2,1,0:T(8,128)(2,1)S(1)} async-done(((bf16[128,8,1024]{2,1,0:T(8,128)(2,1)}), bf16[128,8,1024]{2,1,0:T(8,128)(2,1)S(1)}, u32[]{:S(2)}, u32[]{:S(2)}) %all-to-all-start.1) | async-done | bytes 2097184 | tf_op jit(solution)/shard_map/all_to_all | solution.py:271
  128.9 0.0 copy-done.1
  128.9 0.4 fusion.2
  129.3 0.1 broadcast_in_dim.2
  129.4 14.4 %all_to_all.21 = bf16[16,16,1024]{2,1,0:T(8,128)(2,1)} all-to-all(bf16[16,16,1024]{2,1,0:T(8,128)(2,1)S(1)} %broadcast_in_dim.2), channel_id=1, replica_groups=mesh['wide'=8,'narrow'=16] {'narrow'}, dimensions={0} | all-to-all | bytes 1048576 | tf_op jit(solution)/shard_map/all_to_all | solution.py:271
  143.7 2.2 %proj_parts.1 = bf16[8,256,128]{2,1,0:T(8,128)(2,1)} custom-call(bf16[256,256]{1,0:T(8,128)(2,1)} %inputs_ref.1, bf16[256,1024]{1,0:T(8,128)(2,1)} %bitcast.18), custom_call_target="tpu_custom_call" | custom-call | tf_op jit(solution)/shard_map/proj_parts/pallas_call | solution.py:259
  146.0 5.3 %all-to-all-start.3 = ((bf16[8,256,128]{2,1,0:T(8,128)(2,1)}), bf16[8,256,128]{2,1,0:T(8,128)(2,1)S(1)}, u32[]{:S(2)}, u32[]{:S(2)}) async-start(bf16[8,256,128]{2,1,0:T(8,128)(2,1)} %proj_parts.1), calls=%async_computation.3 | async-start | bytes 1048576 | tf_op jit(solution)/shard_map/all_to_all | solution.py:271
  151.3 0.0 copy-done
  151.3 2.0 %convolution_convert_fusion = bf16[256,256]{1,0:T(8,128)(2,1)} fusion(bf16[256,1024]{1,0:T(8,128)(2,1)} %bitcast.19, bf16[256,1024]{1,0:T(8,128)(2,1)S(1)} %copy-done), kind=kOutput, calls=%fused_computation.2 | convolution fusion | flops 134283264 | bytes 1179648 | tf_op jit(solution)/shard_map/dot_general | solution.py:19
  153.3 7.3 %all-to-all-done.3 = bf16[8,256,128]{2,1,0:T(8,128)(2,1)S(1)} async-done(((bf16[8,256,128]{2,1,0:T(8,128)(2,1)}), bf16[8,256,128]{2,1,0:T(8,128)(2,1)S(1)}, u32[]{:S(2)}, u32[]{:S(2)}) %all-to-all-start.3) | async-done | bytes 524320 | tf_op jit(solution)/shard_map/all_to_all | solution.py:271
  160.7 0.7 convert_reduce_fusion
Async XLA Ops:
  0.6 150.7 %copy-start = (bf16[256,1024]{1,0:T(8,128)(2,1)S(1)}, bf16[256,1024]{1,0:T(8,128)(2,1)}, u32[]{:S(2)}) copy-start(bf16[256,1024]{1,0:T(8,128)(2,1)} %param.15) | copy-start | bytes 1572868
  94.4 34.5 %all-to-all-start.1 = ((bf16[128,8,1024]{2,1,0:T(8,128)(2,1)}), bf16[128,8,1024]{2,1,0:T(8,128)(2,1)S(1)}, u32[]{:S(2)}, u32[]{:S(2)}) async-start(bf16[128,8,1024]{2,1,0:T(8,128)(2,1)} %bitcast.21), calls=%async_computation.1 | async-start | bytes 4194304 | tf_op jit(solution)/shard_map/all_to_all | solution.py:271
  99.5 29.4 %copy-start.1 = (bf16[16,1024]{1,0:T(8,128)(2,1)S(1)}, bf16[16,1024]{1,0:T(8,128)(2,1)}, u32[]{:S(2)}) copy-start(bf16[16,1024]{1,0:T(8,128)(2,1)} %get-tuple-element.22) | copy-start | bytes 98308
  146.0 14.7 %all-to-all-start.3 = ((bf16[8,256,128]{2,1,0:T(8,128)(2,1)}), bf16[8,256,128]{2,1,0:T(8,128)(2,1)S(1)}, u32[]{:S(2)}, u32[]{:S(2)}) async-start(bf16[8,256,128]{2,1,0:T(8,128)(2,1)} %proj_parts.1), calls=%async_computation.3 | async-start | bytes 1048576 | tf_op jit(solution)/shard_map/all_to_all | solution.py:271

commit v3 on v2

v3 whole, which is shorter than its diff:
```python
import functools

import jax
import jax.numpy as jnp
from jax import lax
from jax.experimental import pallas as pl
from jax.experimental.pallas import tpu as pltpu
from jax.sharding import PartitionSpec as P

BF16 = jnp.bfloat16
F32 = jnp.float32
SLOTS = 8
BLOCK = 512
CHUNK = 768
PACK_STEPS = 4
VMEM_LIMIT = 28 * 1024 * 1024


def dot(a, b, dims, **kw):
    return lax.dot_general(a, b, (dims, ((), ())), preferred_element_type=F32, **kw)


NN = ((1,), (0,))
NT = ((1,), (1,))
TN = ((0,), (0,))


def pack_kernel(
    route_hbm, gate_hbm, z_hbm, g_hbm, send, place_ref, route_ref, gate_ref, z_ref, g_ref, sem
):
    pairs = ((route_hbm, route_ref), (gate_hbm, gate_ref), (z_hbm, z_ref), (g_hbm, g_ref))
    loads = [pltpu.make_async_copy(a, b, sem.at[i]) for i, (a, b) in enumerate(pairs)]
    for c in loads:
        c.start()
    tokens, top = route_ref.shape
    experts = 128
    total, twice = send.shape
    width = twice // 2
    for c in loads:
        c.wait()
    routes = route_ref[...]
    gates = gate_ref[...]
    expert_of = lax.broadcasted_iota(jnp.int32, (tokens, experts), 1)
    hits = jnp.zeros((tokens, experts), F32)
    weights = jnp.zeros((tokens, experts), F32)
    for k in range(top):
        same = routes[:, k : k + 1] == expert_of
        hits = jnp.where(same, 1.0, hits)
        weights = jnp.where(same, gates[:, k : k + 1], weights)
    before = lax.broadcasted_iota(jnp.int32, (tokens, tokens), 1) < lax.broadcasted_iota(
        jnp.int32, (tokens, tokens), 0
    )
    rank = dot(before.astype(F32).astype(BF16), hits.astype(BF16), NN)
    rank = jnp.where(hits > 0, rank, -1.0).astype(BF16)
    rows = total // PACK_STEPS
    for p in range(PACK_STEPS):
        r = slice(p * rows, (p + 1) * rows)
        row = lax.broadcasted_iota(jnp.int32, (rows, experts), 0) + p * rows
        expert = lax.broadcasted_iota(jnp.int32, (rows, experts), 1)
        spread = jnp.where((row >> 3) == expert, 1.0, 0.0)
        spread_bf = spread.astype(BF16)
        slot = lax.broadcasted_iota(jnp.int32, (rows, tokens), 0) & (SLOTS - 1)
        chosen = jnp.where(dot(spread_bf, rank, NT) == slot.astype(F32), 1.0, 0.0)
        gate = jnp.sum(
            chosen * dot(spread, weights, NT, precision=lax.Precision.HIGHEST),
            axis=1,
            keepdims=True,
        )
        chosen = chosen.astype(BF16)
        send[r, :width] = dot(chosen, z_ref[...], NN).astype(BF16)
        send[r, width:] = (dot(chosen, g_ref[...], NN) * gate).astype(BF16)
        slot_t = lax.broadcasted_iota(jnp.int32, (tokens, rows), 1) & (SLOTS - 1)
        place_ref[:, r] = jnp.where(
            dot(rank, spread_bf, NT) == slot_t.astype(F32), 1.0, 0.0
        ).astype(BF16)


def pack(routes, gates, z, g):
    tokens, width = z.shape
    total = 128 * SLOTS
    vmem = pl.BlockSpec(memory_space=pltpu.VMEM)
    return pl.pallas_call(
        pack_kernel,
        in_specs=[pl.BlockSpec(memory_space=pltpu.HBM)] * 4,
        out_specs=[vmem, vmem],
        out_shape=[pltpu.VMEM((total, 2 * width), BF16), pltpu.VMEM((tokens, total), BF16)],
        scratch_shapes=[pltpu.VMEM(x.shape, x.dtype) for x in (routes, gates, z, g)]
        + [pltpu.SemaphoreType.DMA((4,))],
        compiler_params=pltpu.CompilerParams(vmem_limit_bytes=VMEM_LIMIT),
        name="pack",
    )(*(pltpu.with_memory_space_constraint(x, pltpu.HBM) for x in (routes, gates, z, g)))


def expert_kernel(
    recv, up, down_hbm, ret_hbm, sq_hbm, hid_hbm,
    down, ret, sq, hid, down_sem, ret_sem, sq_sem, hid_sem,
):
    total, twice = recv.shape
    width = twice // 2
    edges = [*range(0, up.shape[1], CHUNK), up.shape[1]]
    spans = [slice(a, b) for a, b in zip(edges[:-1], edges[1:])]
    weights = [
        pltpu.make_async_copy(down_hbm.at[c, :], down.at[c, :], down_sem.at[n])
        for n, c in enumerate(spans)
    ]
    for w in weights:
        w.start()
    outs = []

    def send_out(src, dst, sem, at):
        outs.append(pltpu.make_async_copy(src.at[at], dst.at[at], sem))
        outs[-1].start()

    for i in range(total // BLOCK):
        r = slice(i * BLOCK, (i + 1) * BLOCK)
        for n, c in enumerate(spans):
            active = jnp.maximum(dot(recv[r, :width], up[:, c], NN), 0.0)
            sq[r, c] = (active * active).astype(BF16)
            if i == 0:
                weights[n].wait()
            act_grad = dot(recv[r, width:], down[c, :], NT)
            hid[r, c] = (act_grad * 2.0 * active).astype(BF16)
            k = i * len(spans) + n
            send_out(sq, sq_hbm, sq_sem.at[k], (r, c))
            send_out(hid, hid_hbm, hid_sem.at[k], (r, c))
        for h in range(2):
            q = slice(i * BLOCK + h * BLOCK // 2, i * BLOCK + (h + 1) * BLOCK // 2)
            ret[q, :] = dot(hid[q, :], up[...], NT).astype(BF16)
            send_out(ret, ret_hbm, ret_sem.at[2 * i + h], (q, slice(None)))
    for c in outs:
        c.wait()


def on_chip(x):
    return pltpu.with_memory_space_constraint(x, pltpu.VMEM)


def expert_pass(recv, up, down):
    total, twice = recv.shape
    width, units = up.shape
    vmem = pl.BlockSpec(memory_space=pltpu.VMEM)
    hbm = pl.BlockSpec(memory_space=pltpu.HBM)
    spans = -(-units // CHUNK)
    blocks = total // BLOCK
    dma = pltpu.SemaphoreType.DMA
    return pl.pallas_call(
        expert_kernel,
        in_specs=[vmem, vmem, hbm],
        out_specs=[hbm] * 3,
        out_shape=[
            pltpu.HBM((total, width), BF16),
            pltpu.HBM((total, units), BF16),
            pltpu.HBM((total, units), BF16),
        ],
        scratch_shapes=[
            pltpu.VMEM((units, width), BF16),
            pltpu.VMEM((total, width), BF16),
            pltpu.VMEM((total, units), BF16),
            pltpu.VMEM((total, units), BF16),
            dma((spans,)),
            dma((2 * blocks,)),
            dma((blocks * spans,)),
            dma((blocks * spans,)),
        ],
        compiler_params=pltpu.CompilerParams(vmem_limit_bytes=VMEM_LIMIT),
        name="expert",
    )(on_chip(recv), on_chip(up), pltpu.with_memory_space_constraint(down, pltpu.HBM))


def weight_kernel(zd_ref, sq_ref, hid_ref, up_ref, down_ref):
    width = zd_ref.shape[1] // 2
    down_ref[0] = dot(sq_ref[...], zd_ref[:, width:], TN).astype(BF16)
    up_ref[0] = dot(zd_ref[:, :width], hid_ref[...], TN).astype(BF16)


def weight_grads(zd, sq, hid):
    total, twice = zd.shape
    width, units = twice // 2, sq.shape[1]
    tile = 384
    return pl.pallas_call(
        weight_kernel,
        grid=(units // tile,),
        in_specs=[
            pl.BlockSpec((total, twice), lambda j: (0, 0)),
            pl.BlockSpec((total, tile), lambda j: (0, j)),
            pl.BlockSpec((total, tile), lambda j: (0, j)),
        ],
        out_specs=[
            pl.BlockSpec((1, width, tile), lambda j: (0, 0, j)),
            pl.BlockSpec((1, tile, width), lambda j: (0, j, 0)),
        ],
        out_shape=[
            jax.ShapeDtypeStruct((1, width, units), BF16),
            jax.ShapeDtypeStruct((1, units, width), BF16),
        ],
        compiler_params=pltpu.CompilerParams(vmem_limit_bytes=2 * VMEM_LIMIT),
        cost_estimate=pl.CostEstimate(
            flops=4 * total * width * units, transcendentals=0, bytes_accessed=8 * width * units
        ),
        name="weight_grads",
    )(zd, sq, hid)


def part_kernel(inputs_ref, piece_ref, parts_ref):
    n_parts, _, columns = parts_ref.shape
    acc = dot(inputs_ref[...], piece_ref[...], TN)
    for p in range(n_parts):
        parts_ref[p] = acc[:, p * columns : (p + 1) * columns].astype(BF16)


def proj_parts(inputs, piece, n_parts):
    vmem = pl.BlockSpec(memory_space=pltpu.VMEM)
    return pl.pallas_call(
        part_kernel,
        in_specs=[vmem, vmem],
        out_specs=vmem,
        out_shape=jax.ShapeDtypeStruct(
            (n_parts, inputs.shape[1], piece.shape[1] // n_parts), BF16
        ),
        compiler_params=pltpu.CompilerParams(vmem_limit_bytes=VMEM_LIMIT),
        name="proj_parts",
    )(on_chip(inputs), on_chip(piece))


def exchange(x, axes):
    return lax.all_to_all(x, axes, split_axis=0, concat_axis=0, tiled=True)


def on_device(
    latent_in, latent_grad, route_ids, gate_values, up_weight, down_weight, inputs, proj_weight
):
    n_wide = lax.axis_size("wide")
    n_narrow = lax.axis_size("narrow")
    experts = n_wide * n_narrow
    both = ("wide", "narrow")
    tokens, width = latent_in.shape
    send, place = pack(route_ids, gate_values, latent_in, latent_grad)
    recv = exchange(send.reshape(experts, SLOTS, 2 * width), both)
    recv = recv.reshape(experts * SLOTS, 2 * width)
    rows, sq, hid = expert_pass(recv, up_weight[0], down_weight[0])
    returned = exchange(rows.reshape(experts, SLOTS, width), both)
    grad_up, grad_down = weight_grads(recv, sq, hid)
    returned, grad_up, grad_down = lax.optimization_barrier((returned, grad_up, grad_down))
    token_grad = dot(place, returned.reshape(experts * SLOTS, width), NN).astype(BF16)
    copies = jnp.broadcast_to(token_grad[None], (n_narrow, tokens, width))
    piece = exchange(copies, "narrow").reshape(n_narrow * tokens, width)
    parts = exchange(proj_parts(inputs, piece, n_wide), "wide")
    grad_proj = jnp.sum(parts.astype(F32), axis=0)
    grad_inputs = dot(piece, proj_weight, NT).astype(BF16)
    return (grad_up, grad_down, grad_inputs, grad_proj)


def solution(mesh):
    placed = (
        P(("wide", "narrow"), None),
        P(("wide", "narrow"), None),
        P(("wide", "narrow"), None),
        P(("wide", "narrow"), None),
        P(("wide", "narrow"), None, None),
        P(("wide", "narrow"), None, None),
        P("wide", "narrow"),
        P("narrow", None),
    )
    return jax.shard_map(
        on_device,
        mesh=mesh,
        in_specs=placed,
        out_specs=(
            P(("wide", "narrow"), None, None),
            P(("wide", "narrow"), None, None),
            P("wide", "narrow"),
            P("narrow", "wide"),
        ),
        check_vma=False,
    )
```

time: 162 us -> 155 us (0.957)
  Pallas kernels: 51.3 us -> 44.7 us
    pallas_call x2, Pallas kernels: 30.6 us -> 25.2 us  [the longest x1 22 us: expert_pass(): pl.pallas_call(expert_kernel, in_specs=[vmem, vmem, hbm], out_specs=[hbm]...]
  transfers between devices with their start and end apart: 2 -> 2, of which waited for: 2 -> 2; matrix products, arithmetic and copies ran while one was open for 1% -> 1% of each run, Pallas kernels for 11% -> 12%
where the time goes in v3:
time: 155 us; the launch traced here: 154 us
  blocking collectives  77 us (50%)
  Pallas kernels  44.7 us (29%)
  waiting for transfers between devices  19.4 us (13%)
  starting transfers between devices  10.4 us (7%)
    all_to_all x2, blocking collectives, exchange(): return lax.all_to_all(x, axes, split_axis=0, concat_axis=0, tiled=True)  77 us
    pallas_call x1, Pallas kernels, expert_pass(): pl.pallas_call(expert_kernel, in_specs=[vmem, vmem, hbm], out_specs=[hbm]...  22 us
    all_to_all x2, waiting for transfers between devices, exchange(): return lax.all_to_all(x, axes, split_axis=0, concat_axis=0, tiled=True)  19.4 us
    pallas_call x1, Pallas kernels, weight_grads(): pl.pallas_call(weight_kernel, grid=(units // tile,), in_specs=[pl.BlockSp...  18.4 us
    all_to_all x2, starting transfers between devices, exchange(): return lax.all_to_all(x, axes, split_axis=0, concat_axis=0, tiled=True)  10.4 us
    pallas_call x1, Pallas kernels, pack(): pl.pallas_call(pack_kernel, in_specs=[pl.BlockSpec(memory_space=pltpu.HBM...  3.17 us
  transfers between devices with their start and end apart: 2, of which 2 were waited for; matrix products, arithmetic and copies ran while one was open for 1% of the time, Pallas kernels for 12%

profile of v3, /device:TPU:1, one launch (start us, length us, event | category | flops | bytes accessed | tf_op | source)
XLA Modules:
  0.0 154.4 jit_solution(6495361965459933252)
XLA Ops:
  0.6 0.0 copy-start
  0.6 3.2 %pack.1 = (bf16[1024,2048]{1,0:T(8,128)(2,1)S(1)}, bf16[16,1024]{1,0:T(8,128)(2,1)S(1)}) custom-call(s32[16,22]{1,0:T(8,128)} %route_hbm.1, f32[16,22]{1,0:T(8,128)} %gate_hbm.1, bf16[16,1024]{1,0:T(8,128)(2,1)} %z_hbm.1, bf16[16,1024]{1,0:T(8,128)(2,1)} %g_hbm.1), custom_call_target="tpu_custom_call" | custom-call | tf_op jit(solution)/shard_map/pack/pallas_call | solution.py:82
  3.8 0.0 copy-start.2
  3.8 62.8 %all_to_all.20 = bf16[128,8,2048]{2,1,0:T(8,128)(2,1)S(1)} all-to-all(bf16[128,8,2048]{2,1,0:T(8,128)(2,1)S(1)} %bitcast.19), channel_id=1, replica_groups=mesh['wide'=8,'narrow'=16] {'wide','narrow'}, dimensions={0} | all-to-all | bytes 8388608 | tf_op jit(solution)/shard_map/all_to_all | solution.py:226
  66.6 0.0 copy-start.1
  66.6 0.0 copy-done.2
  66.6 22.0 %expert.1 = (bf16[1024,1024]{1,0:T(8,128)(2,1)}, bf16[1024,2688]{1,0:T(8,128)(2,1)}, bf16[1024,2688]{1,0:T(8,128)(2,1)}) custom-call(bf16[1024,2048]{1,0:T(8,128)(2,1)S(1)} %bitcast.14, bf16[1024,2688]{1,0:T(8,128)(2,1)S(1)} %bitcast.16, bf16[2688,1024]{1,0:T(8,128)(2,1)} %bitcast.20), custom_call_target="tpu_custom_call" | custom-call | tf_op jit(solution)/shard_map/expert/pallas_call | solution.py:146
  88.7 0.0 copy-done.1
  88.7 5.1 %all-to-all-start.1 = ((bf16[128,8,1024]{2,1,0:T(8,128)(2,1)}), bf16[128,8,1024]{2,1,0:T(8,128)(2,1)S(1)}, u32[]{:S(2)}, u32[]{:S(2)}) async-start(bf16[128,8,1024]{2,1,0:T(8,128)(2,1)} %bitcast.21), calls=%async_computation.1 | async-start | bytes 4194304 | tf_op jit(solution)/shard_map/all_to_all | solution.py:226
  93.8 0.0 copy-start.3
  93.8 18.4 %weight_grads.1 = (bf16[1,1024,2688]{2,1,0:T(8,128)(2,1)}, bf16[1,2688,1024]{2,1,0:T(8,128)(2,1)}) custom-call(bf16[1024,2048]{1,0:T(8,128)(2,1)} %bitcast.15, bf16[1024,2688]{1,0:T(8,128)(2,1)} %get-tuple-element.16.sq_ref, bf16[1024,2688]{1,0:T(8,128)(2,1)} %get-tuple-element.17.hid_ref), custom_call_target="tpu_custom_call" | custom-call | flops 11274289152 | bytes 22020096 | tf_op jit(solution)/shard_map/weight_grads/pallas_call | solution.py:180
  112.2 11.0 %all-to-all-done.1 = bf16[128,8,1024]{2,1,0:T(8,128)(2,1)S(1)} async-done(((bf16[128,8,1024]{2,1,0:T(8,128)(2,1)}), bf16[128,8,1024]{2,1,0:T(8,128)(2,1)S(1)}, u32[]{:S(2)}, u32[]{:S(2)}) %all-to-all-start.1) | async-done | bytes 2097184 | tf_op jit(solution)/shard_map/all_to_all | solution.py:226
  123.2 0.4 fusion.2
  123.6 0.1 broadcast_in_dim.2
  123.6 14.2 %all_to_all.21 = bf16[16,16,1024]{2,1,0:T(8,128)(2,1)S(1)} all-to-all(bf16[16,16,1024]{2,1,0:T(8,128)(2,1)S(1)} %broadcast_in_dim.2), channel_id=1, replica_groups=mesh['wide'=8,'narrow'=16] {'narrow'}, dimensions={0} | all-to-all | bytes 1048576 | tf_op jit(solution)/shard_map/all_to_all | solution.py:226
  137.9 0.0 copy-done.3
  137.9 1.1 proj_parts.1
  139.0 5.3 %all-to-all-start.3 = ((bf16[8,256,128]{2,1,0:T(8,128)(2,1)}), bf16[8,256,128]{2,1,0:T(8,128)(2,1)S(1)}, u32[]{:S(2)}, u32[]{:S(2)}) async-start(bf16[8,256,128]{2,1,0:T(8,128)(2,1)} %proj_parts.1), calls=%async_computation.3 | async-start | bytes 1048576 | tf_op jit(solution)/shard_map/all_to_all | solution.py:226
  144.3 0.0 copy-done
  144.3 1.0 convolution_convert_fusion
  145.3 8.4 %all-to-all-done.3 = bf16[8,256,128]{2,1,0:T(8,128)(2,1)S(1)} async-done(((bf16[8,256,128]{2,1,0:T(8,128)(2,1)}), bf16[8,256,128]{2,1,0:T(8,128)(2,1)S(1)}, u32[]{:S(2)}, u32[]{:S(2)}) %all-to-all-start.3) | async-done | bytes 524320 | tf_op jit(solution)/shard_map/all_to_all | solution.py:226
  153.7 0.7 convert_reduce_fusion
Async XLA Ops:
  0.6 143.7 %copy-start = (bf16[256,1024]{1,0:T(8,128)(2,1)S(1)}, bf16[256,1024]{1,0:T(8,128)(2,1)}, u32[]{:S(2)}) copy-start(bf16[256,1024]{1,0:T(8,128)(2,1)} %param.15) | copy-start | bytes 1572868
  3.8 62.8 %copy-start.2 = (bf16[1,1024,2688]{2,1,0:T(8,128)(2,1)S(1)}, bf16[1,1024,2688]{2,1,0:T(8,128)(2,1)}, u32[]{:S(2)}) copy-start(bf16[1,1024,2688]{2,1,0:T(8,128)(2,1)} %param.12) | copy-start | bytes 16515076
  66.6 22.0 %copy-start.1 = (bf16[128,8,2048]{2,1,0:T(8,128)(2,1)}, bf16[128,8,2048]{2,1,0:T(8,128)(2,1)S(1)}, u32[]{:S(2)}) copy-start(bf16[128,8,2048]{2,1,0:T(8,128)(2,1)S(1)} %all_to_all.20) | copy-start | bytes 12582916
  88.7 34.5 %all-to-all-start.1 = ((bf16[128,8,1024]{2,1,0:T(8,128)(2,1)}), bf16[128,8,1024]{2,1,0:T(8,128)(2,1)S(1)}, u32[]{:S(2)}, u32[]{:S(2)}) async-start(bf16[128,8,1024]{2,1,0:T(8,128)(2,1)} %bitcast.21), calls=%async_computation.1 | async-start | bytes 4194304 | tf_op jit(solution)/shard_map/all_to_all | solution.py:226
  93.8 44.1 %copy-start.3 = (bf16[256,256]{1,0:T(8,128)(2,1)S(1)}, bf16[256,256]{1,0:T(8,128)(2,1)}, u32[]{:S(2)}) copy-start(bf16[256,256]{1,0:T(8,128)(2,1)} %inputs_ref.1) | copy-start | bytes 393220
  139.0 14.7 %all-to-all-start.3 = ((bf16[8,256,128]{2,1,0:T(8,128)(2,1)}), bf16[8,256,128]{2,1,0:T(8,128)(2,1)S(1)}, u32[]{:S(2)}, u32[]{:S(2)}) async-start(bf16[8,256,128]{2,1,0:T(8,128)(2,1)} %proj_parts.1), calls=%async_computation.3 | async-start | bytes 1048576 | tf_op jit(solution)/shard_map/all_to_all | solution.py:226
